TPU v7x, 32 devices: a whole 2x2x4 slice. The times are simulated.
32 devices in a mesh: segment: 2 (over core), dp: 4 (over y, x), mp: 4 (over z).
Axes of the slice: x: 2, y: 2, z: 4, core: 2. Of those that a mesh axis runs over, the one named last changes fastest.
Arguments:
- token_ids: int32 [2, 256], replicated, may hold values from 0 to 32767
- table: bfloat16 [32768, 8192], P('dp', 'mp'), may hold values from -6 to 6
- w_up: bfloat16 [2, 8192, 32768], P('segment', 'mp', 'dp'), may hold values from -0.0625 to 0.0625
- w_down: bfloat16 [2, 32768, 8192], P('segment', 'dp', 'mp'), may hold values from -0.03125 to 0.03125
- cotangent: bfloat16 [2, 256, 8192], P(None, 'dp', 'mp'), may hold values from -6 to 6
Outputs:
- acts: bfloat16 [2, 2, 256, 8192], P('segment', None, 'dp', 'mp')
- grads: bfloat16 [2, 2, 256, 8192], P('segment', None, 'dp', 'mp')
All inputs are finite; a program needn't handle non-finite values.
Results may differ from a plain program's by a relative error of at most 0.018.
Values may be sent and summed in bfloat16 or wider, within the bound.
A program may use at most 192 MiB of HBM per device.

v0:
```python
import functools

import jax
import jax.numpy as jnp
from jax import lax
from jax.experimental import pallas as pl
from jax.experimental.pallas import tpu as pltpu
from jax.sharding import PartitionSpec as P

CHUNK = 256
SKEW = 1
LAG = 2
BLOCK = 512
VMEM_BYTES = 67_043_328

root_coef = 0.7978845608028654


def gelu_value(value):
    return 0.5 * value * (1.0 + jnp.tanh(root_coef * (value + 0.044715 * value * value * value)))


def gelu_slope(value):
    inner = jnp.tanh(root_coef * (value + 0.044715 * value * value * value))
    return 0.5 * (1.0 + inner) + 0.5 * value * (1.0 - inner * inner) * root_coef * (
        1.0 + 0.134145 * value * value
    )


def relay_kernel(
    count_dp, count_mp, micros, chunks, width,
    emb_ref, cot_ref, up_ref, down_ref, acts_ref, grads_ref,
    xin, rs, ag, acc, up_buf, down_buf, stage, inbox, part, total,
    rs_send, rs_recv, ag_send, ag_recv, fin_send, fin_recv, x_send, x_recv, emb_send, emb_recv, w_sem,
):
    seg, d, p = lax.axis_index("segment"), lax.axis_index("dp"), lax.axis_index("mp")
    n = count_mp
    rows, model = xin.shape[1], xin.shape[2]
    local = rows // count_dp
    all_chunks = micros * chunks
    half = chunks * width
    block = min(BLOCK, model)
    own = pl.ds(pl.multiple_of(d * local, local), local)

    def rem_dp(value):
        return lax.rem(value, count_dp)

    def place(h):
        return p + h * (n - 1 - 2 * p)

    barrier = pltpu.get_barrier_semaphore()

    def greet(target):
        pl.semaphore_signal(barrier, inc=1, device_id=target, device_id_type=pl.DeviceIdType.MESH)

    for i in range(1, count_mp):
        greet((seg, d, lax.rem(p + i, count_mp)))
    for i in range(1, count_dp):
        greet((seg, rem_dp(d + i), p))
    for i in range(count_dp):
        greet((1 - seg, rem_dp(d + i), p))
    pl.semaphore_wait(barrier, count_mp - 1 + 2 * count_dp - 1)

    def remote(src, dst, send, recv, target):
        return pltpu.make_async_remote_copy(
            src_ref=src, dst_ref=dst, send_sem=send, recv_sem=recv,
            device_id=target, device_id_type=pl.DeviceIdType.MESH,
        )

    def rs_copy(i, h, k):
        nxt = lax.rem(p + 1 - 2 * h + n, n)
        return remote(rs.at[i, h, k], rs.at[i, h, k], rs_send.at[i, h, k], rs_recv.at[i, h, k], (seg, d, nxt))

    def ag_copy(i, h, k):
        nxt = lax.rem(p - 1 + 2 * h + n, n)
        return remote(ag.at[i, h, k], ag.at[i, h, k], ag_send.at[i, h, k], ag_recv.at[i, h, k], (seg, d, nxt))

    def fin_copy(e, src_rank, dst_rank):
        return remote(
            stage.at[pl.ds(pl.multiple_of(dst_rank * local, local), local)], inbox.at[e, src_rank],
            fin_send.at[e, dst_rank], fin_recv.at[e, src_rank], (seg, dst_rank, p),
        )

    def x_copy(src, i, src_rank, dst_rank, dst_seg):
        return remote(
            src, xin.at[i, pl.ds(pl.multiple_of(src_rank * local, local), local)],
            x_send.at[i, dst_rank], x_recv.at[i, src_rank], (dst_seg, dst_rank, p),
        )

    def emb_copy(m, src_rank, dst_rank):
        return remote(
            emb_ref.at[pl.ds(pl.multiple_of(dst_rank * local, local), local)], inbox.at[micros + m, src_rank],
            emb_send.at[dst_rank], emb_recv.at[m, src_rank], (0, dst_rank, p),
        )

    def wait_input(i, m):
        index = i * micros + m
        for j in range(count_dp):
            other = rem_dp(d + j)
            if i == 0 and j == 0:
                continue
            x_copy(acts_ref.at[0], index, other, other, seg).wait_recv()

    def finish_start(g, m):
        e = g * micros + m
        for j in range(count_dp):
            dst = rem_dp(d + j + 1)
            at = pl.ds(pl.multiple_of(dst * local, local), local)
            if j < count_dp - 1:
                stage[at] = acc[m, at].astype(stage.dtype)
                fin_copy(e, d, dst).start()

    def finish_end(g, m, out_ref):
        e = g * micros + m
        total[...] = xin[e, own].astype(jnp.float32) + acc[m, own]
        for j in range(1, count_dp):
            src = rem_dp(d + j)
            fin_copy(e, src, src).wait_recv()
            total[...] += inbox[e, src].astype(jnp.float32)
        out_ref[m] = total[...].astype(out_ref.dtype)
        if g == 0:
            for j in range(count_dp):
                x_copy(out_ref.at[m], micros + m, d, rem_dp(d + j), 1 - seg).start()
        for j in range(1, count_dp):
            fin_copy(e, d, rem_dp(d + j)).wait_send()

    def weight_copy(use, kind, h, k, slot):
        base = pl.multiple_of(h * half + lax.rem(k, chunks) * width, width)
        sem = w_sem.at[use, h, slot]
        if kind == "up":
            return pltpu.make_async_copy(up_ref.at[:, pl.ds(base, width)], up_buf.at[use * 4 + h * 2 + slot], sem)
        return pltpu.make_async_copy(down_ref.at[pl.ds(base, width), :], down_buf.at[h * 2 + slot], sem)

    def stream(i, a, first, second, epilogue, hooks):
        base = SKEW * (n - 1) if first is not None else 0
        steps = all_chunks + (SKEW * (n - 1) if first is not None else 0) + (SKEW * (n - 1) if second is not None else 0)

        def rs_index(h, t):
            return t - SKEW * place(h)

        def ag_index(h, t):
            return t - base - SKEW * (n - 1 - place(h))

        def valid(k):
            return (k >= 0) & (k < all_chunks)

        def prefetch(t, slot):
            def half_step(h, carry):
                if first is not None:
                    k = rs_index(h, t)

                    @pl.when(valid(k))
                    def _():
                        weight_copy(0, first, h, k, slot).start()

                if second is not None:
                    ka = ag_index(h, t)

                    @pl.when(valid(ka))
                    def _():
                        weight_copy(1, second, h, ka, slot).start()

                return carry

            lax.fori_loop(0, 2, half_step, 0)

        def forward(h, t):
            k, q = ag_index(h, t), place(h)

            @pl.when(valid(k))
            def _():
                @pl.when(q < n - 1)
                def _():
                    ag_copy(a, h, k).wait_recv()

                moves = (q > 0) if first is None else (q > 0) & (q < n - 1)

                @pl.when(moves)
                def _():
                    ag_copy(a, h, k).start()

        def reduce(h, t, slot):
            k, q = rs_index(h, t), place(h)

            @pl.when(valid(k))
            def _():
                m = lax.div(k, chunks)
                weight_copy(0, first, h, k, slot).wait()
                x = xin[i * micros + m]
                if first == "up":
                    part[...] = jnp.dot(x, up_buf[h * 2 + slot], preferred_element_type=jnp.float32)
                else:
                    part[...] = lax.dot_general(
                        x, down_buf[h * 2 + slot], (((1,), (1,)), ((), ())), preferred_element_type=jnp.float32
                    )

                @pl.when(q > 0)
                def _():
                    rs_copy(i, h, k).wait_recv()
                    part[...] += rs[i, h, k].astype(jnp.float32)

                @pl.when(q < n - 1)
                def _():
                    rs[i, h, k] = part[...].astype(rs.dtype)
                    rs_copy(i, h, k).start()

                @pl.when(q == n - 1)
                def _():
                    epilogue(h, k)
                    if second is not None:
                        ag_copy(a, h, k).start()

        def accumulate(h, t, slot):
            k = ag_index(h, t)

            @pl.when(valid(k))
            def _():
                m = lax.div(k, chunks)
                weight_copy(1, second, h, k, slot).wait()

                def columns(b, carry):
                    at = pl.ds(pl.multiple_of(b * block, block), block)
                    if second == "down":
                        acc[m, :, at] += jnp.dot(
                            ag[a, h, k], down_buf[h * 2 + slot, :, at], preferred_element_type=jnp.float32
                        )
                    else:
                        acc[m, :, at] += lax.dot_general(
                            ag[a, h, k], up_buf[4 + h * 2 + slot, at, :], (((1,), (1,)), ((), ())),
                            preferred_element_type=jnp.float32,
                        )
                    return carry

                lax.fori_loop(0, model // block, columns, 0)

        def step(t, carry):
            slot = lax.rem(t, 2)

            @pl.when(t + 1 < steps)
            def _():
                prefetch(t + 1, 1 - slot)

            for m in range(micros):

                @pl.when(t == m * chunks)
                def _():
                    if first is not None:
                        wait_input(i, m)
                    if second is not None:
                        acc[m] = jnp.zeros(acc.shape[1:], acc.dtype)

            def both(body):
                def run(h, inner):
                    body(h)
                    return inner

                lax.fori_loop(0, 2, run, 0)

            if second is not None:
                both(lambda h: forward(h, t))
            if first is not None:
                both(lambda h: reduce(h, t, slot))
            if second is not None:
                both(lambda h: accumulate(h, t, slot))
            for when, act in hooks:

                @pl.when(t == when)
                def _():
                    act()

            return carry

        prefetch(0, 0)
        lax.fori_loop(0, steps, step, 0)

    def ends(m, span):
        return (m + 1) * chunks - 1 + span * SKEW * (n - 1)

    def finish_hooks(g, span, out_ref):
        hooks = []
        for m in range(micros - 1):
            hooks.append((ends(m, span), functools.partial(finish_start, g, m)))
            hooks.append((ends(m, span) + LAG, functools.partial(finish_end, g, m, out_ref)))
        return hooks

    def send_forward(h, k):
        ag[0, h, k] = gelu_value(part[...]).astype(ag.dtype)
        rs[0, h, k] = part[...].astype(rs.dtype)

    def send_backward(h, k):
        ag[1, h, k] = (gelu_slope(rs[0, h, k].astype(jnp.float32)) * part[...]).astype(ag.dtype)

    def keep(h, k):
        rs[0, h, k] = part[...].astype(rs.dtype)

    def send_turn(h, k):
        pre = part[...]
        ag[0, h, k] = (gelu_slope(pre) * rs[0, h, k].astype(jnp.float32)).astype(ag.dtype)
        ag[1, h, k] = gelu_value(pre).astype(ag.dtype)

    last = micros - 1

    @pl.when(seg == 0)
    def _():
        for j in range(1, count_dp):
            emb_copy(0, d, rem_dp(d + j)).start()
        for m in range(micros):
            if m == 0:
                total[...] = emb_ref[own].astype(jnp.float32)
            else:
                total[...] = jnp.zeros(total.shape, total.dtype)
            for j in range(count_dp):
                src = rem_dp(d + j)
                if m == 0 and j == 0:
                    continue
                emb_copy(m, src, src).wait_recv()
                total[...] += inbox[micros + m, src].astype(jnp.float32)
            xin[m, own] = total[...].astype(xin.dtype)
            for j in range(1, count_dp):
                x_copy(xin.at[m, own], m, d, rem_dp(d + j), seg).start()
        stream(0, 0, "up", "down", send_forward, finish_hooks(0, 2, acts_ref))
        finish_start(0, last)
        finish_end(0, last, acts_ref)
        stream(1, 1, "down", "up", send_backward, finish_hooks(1, 2, grads_ref))
        finish_start(1, last)
        finish_end(1, last, grads_ref)
        for j in range(1, count_dp):
            emb_copy(0, d, rem_dp(d + j)).wait_send()

    @pl.when(seg == 1)
    def _():
        for j in range(count_dp):
            emb_copy(1, d, rem_dp(d + j)).start()
        for m in range(micros):
            xin[m, own] = cot_ref[m]
            for j in range(1, count_dp):
                x_copy(cot_ref.at[m], m, d, rem_dp(d + j), seg).start()
        stream(0, 0, "down", None, keep, [])
        stream(1, 0, "up", "up", send_turn, finish_hooks(0, 2, grads_ref))
        finish_start(0, last)
        stream(1, 1, None, "down", None, [(LAG, functools.partial(finish_end, 0, last, grads_ref))] + finish_hooks(1, 1, acts_ref))
        finish_start(1, last)
        finish_end(1, last, acts_ref)
        for j in range(count_dp):
            emb_copy(1, d, rem_dp(d + j)).wait_send()

    def drain(k, carry):
        for i in range(2):
            for h in range(2):

                @pl.when(place(h) < n - 1)
                def _():
                    rs_copy(i, h, k).wait_send()

                @pl.when(place(h) > 0)
                def _():
                    ag_copy(i, h, k).wait_send()

        return carry

    lax.fori_loop(0, all_chunks, drain, 0)
    for m in range(micros):
        for j in range(count_dp):
            if j > 0:
                x_copy(cot_ref.at[m], m, d, rem_dp(d + j), seg).wait_send()
            x_copy(cot_ref.at[m], micros + m, d, rem_dp(d + j), 1 - seg).wait_send()


def relay(emb, cotangent, w_up, w_down, count_dp, count_mp):
    micros, local, model = cotangent.shape
    rows = emb.shape[0]
    hidden = w_up.shape[1]
    chunks = max(1, hidden // 2 // CHUNK)
    width = hidden // 2 // chunks
    all_chunks = micros * chunks
    low, full = jnp.bfloat16, jnp.float32
    vmem = pl.BlockSpec(memory_space=pltpu.VMEM)
    hbm = pl.BlockSpec(memory_space=pl.ANY)
    dma = pltpu.SemaphoreType.DMA
    out = jax.ShapeDtypeStruct((micros, local, model), low)
    return pl.pallas_call(
        functools.partial(relay_kernel, count_dp, count_mp, micros, chunks, width),
        out_shape=(out, out),
        in_specs=[vmem, vmem, hbm, hbm],
        out_specs=(vmem, vmem),
        scratch_shapes=[
            pltpu.VMEM((2 * micros, rows, model), low),
            pltpu.VMEM((2, 2, all_chunks, rows, width), low),
            pltpu.VMEM((2, 2, all_chunks, rows, width), low),
            pltpu.VMEM((micros, rows, model), full),
            pltpu.VMEM((8, model, width), low),
            pltpu.VMEM((4, width, model), low),
            pltpu.VMEM((rows, model), low),
            pltpu.VMEM((2 * micros, count_dp, local, model), low),
            pltpu.VMEM((rows, width), full),
            pltpu.VMEM((local, model), full),
            dma((2, 2, all_chunks)),
            dma((2, 2, all_chunks)),
            dma((2, 2, all_chunks)),
            dma((2, 2, all_chunks)),
            dma((2 * micros, count_dp)),
            dma((2 * micros, count_dp)),
            dma((2 * micros, count_dp)),
            dma((2 * micros, count_dp)),
            dma((count_dp,)),
            dma((micros, count_dp)),
            dma((2, 2, 2)),
        ],
        compiler_params=pltpu.CompilerParams(
            collective_id=0, has_side_effects=True, vmem_limit_bytes=VMEM_BYTES
        ),
    )(emb, cotangent, w_up, w_down)


def on_device(token_ids, table, w_up, w_down, cotangent):
    table_rows = table.shape[0]
    ids = lax.dynamic_index_in_dim(token_ids, lax.axis_index("segment"), 0, keepdims=False)
    picked = ids - lax.axis_index("dp") * table_rows
    inside = (picked >= 0) & (picked < table_rows)
    fetched = jnp.take(table, jnp.clip(picked, 0, table_rows - 1), axis=0, mode="clip")
    emb = jnp.where(inside[:, None], fetched, jnp.zeros_like(fetched))
    acts, grads = relay(emb, cotangent, w_up[0], w_down[0], lax.axis_size("dp"), lax.axis_size("mp"))
    return acts[None], grads[None]


def solution(mesh):
    return jax.shard_map(
        on_device,
        mesh=mesh,
        in_specs=(
            P(),
            P("dp", "mp"),
            P("segment", "mp", "dp"),
            P("segment", "dp", "mp"),
            P(None, "dp", "mp"),
        ),
        out_specs=(P("segment", None, "dp", "mp"), P("segment", None, "dp", "mp")),
        check_vma=False,
    )
```

profile of v0, /device:TPU:0, one launch (start us, length us, event | category | flops | bytes accessed | tf_op | source)
XLA Modules:
  0.0 544.1 jit_solution(1833926344597118213)
XLA Ops:
  0.6 0.7 and_reduce_fusion
  1.3 0.7 broadcast_clamp_fusion
  2.0 10.0 %gather_fusion = bf16[256,2048]{1,0:T(8,128)(2,1)S(1)} fusion(bf16[8192,2048]{1,0:T(8,128)(2,1)} %param.6, s32[1024]{0:T(1024)S(1)} %pad_clamp_fusion), kind=kCustom, calls=%fused_computation | custom fusion | bytes 2098176 | tf_op jit(solution)/shard_map/jit(_take)/gather | solution.py:420
  12.1 1.1 broadcast_select_fusion.emb_ref
  13.2 527.1 %shard_map.68 = (bf16[2,64,2048]{2,1,0:T(8,128)(2,1)}, bf16[2,64,2048]{2,1,0:T(8,128)(2,1)}) custom-call(bf16[256,2048]{1,0:T(8,128)(2,1)} %broadcast_select_fusion.emb_ref, bf16[2,64,2048]{2,1,0:T(8,128)(2,1)} %cot_ref.1, bf16[2048,8192]{1,0:T(8,128)(2,1)} %bitcast.5, bf16[8192,2048]{1,0:T(8,128)(2,1)} %bitcast.6), custom_call_target="tpu_custom_call" | custom-call | tf_op jit(solution)/shard_map/pallas_call | solution.py:381
  540.3 1.9 copy.9
  542.2 1.9 copy.10
  (1 shorter events, 0.0 us)
where the time goes:
time: 545 us; the launch traced here: 544 us
  Pallas kernels  527 us (97%)
  local copies, waits for them, and re-layouts  13.8 us (3%)
    pallas_call x1, Pallas kernels, relay(): pl.pallas_call(functools.partial(relay_kernel, count_dp, count_mp, micros...  527 us

commit v1 on v0

--- a/solution.py
+++ b/solution.py
@@ -8,7 +8,8 @@
 from jax.sharding import PartitionSpec as P
 
 CHUNK = 256
-SKEW = 1
+SPLIT = 2
+SKEW = 2
 LAG = 2
 BLOCK = 512
 VMEM_BYTES = 67_043_328
@@ -28,7 +29,7 @@
 
 
 def relay_kernel(
-    count_dp, count_mp, micros, chunks, width,
+    count_dp, count_mp, split, chunks, width,
     emb_ref, cot_ref, up_ref, down_ref, acts_ref, grads_ref,
     xin, rs, ag, acc, up_buf, down_buf, stage, inbox, part, total,
     rs_send, rs_recv, ag_send, ag_recv, fin_send, fin_recv, x_send, x_recv, emb_send, emb_recv, w_sem,
@@ -36,6 +37,8 @@
     seg, d, p = lax.axis_index("segment"), lax.axis_index("dp"), lax.axis_index("mp")
     n = count_mp
     rows, model = xin.shape[1], xin.shape[2]
+    micros = acc.shape[0]
+    lag = min(LAG, chunks - 1)
     local = rows // count_dp
     all_chunks = micros * chunks
     half = chunks * width
@@ -88,10 +91,25 @@
         )
 
     def emb_copy(m, src_rank, dst_rank):
+        within = m % split
         return remote(
-            emb_ref.at[pl.ds(pl.multiple_of(dst_rank * local, local), local)], inbox.at[micros + m, src_rank],
-            emb_send.at[dst_rank], emb_recv.at[m, src_rank], (0, dst_rank, p),
+            emb_ref.at[pl.ds(pl.multiple_of(within * rows + dst_rank * local, local), local)],
+            inbox.at[micros + m, src_rank],
+            emb_send.at[within, dst_rank], emb_recv.at[m, src_rank], (0, dst_rank, p),
         )
+
+    def embed_end(m):
+        if m < split:
+            total[...] = emb_ref[pl.ds(pl.multiple_of(m * rows + d * local, local), local)].astype(jnp.float32)
+        else:
+            total[...] = jnp.zeros(total.shape, total.dtype)
+        for j in range(1 if m < split else 0, count_dp):
+            src = rem_dp(d + j)
+            emb_copy(m, src, src).wait_recv()
+            total[...] += inbox[micros + m, src].astype(jnp.float32)
+        xin[m, own] = total[...].astype(xin.dtype)
+        for j in range(1, count_dp):
+            x_copy(xin.at[m, own], m, d, rem_dp(d + j), seg).start()
 
     def wait_input(i, m):
         index = i * micros + m
@@ -131,7 +149,7 @@
             return pltpu.make_async_copy(up_ref.at[:, pl.ds(base, width)], up_buf.at[use * 4 + h * 2 + slot], sem)
         return pltpu.make_async_copy(down_ref.at[pl.ds(base, width), :], down_buf.at[h * 2 + slot], sem)
 
-    def stream(i, a, first, second, epilogue, hooks):
+    def stream(i, a, first, second, epilogue, finish=None, hooks=()):
         base = SKEW * (n - 1) if first is not None else 0
         steps = all_chunks + (SKEW * (n - 1) if first is not None else 0) + (SKEW * (n - 1) if second is not None else 0)
 
@@ -240,14 +258,13 @@
             def _():
                 prefetch(t + 1, 1 - slot)
 
-            for m in range(micros):
-
-                @pl.when(t == m * chunks)
-                def _():
-                    if first is not None:
-                        wait_input(i, m)
-                    if second is not None:
-                        acc[m] = jnp.zeros(acc.shape[1:], acc.dtype)
+            @pl.when((lax.rem(t, chunks) == 0) & (t < all_chunks))
+            def _():
+                m = lax.div(t, chunks)
+                if first is not None:
+                    wait_input(i, m)
+                if second is not None:
+                    acc[m] = jnp.zeros(acc.shape[1:], acc.dtype)
 
             def both(body):
                 def run(h, inner):
@@ -262,6 +279,20 @@
                 both(lambda h: reduce(h, t, slot))
             if second is not None:
                 both(lambda h: accumulate(h, t, slot))
+            if finish is not None:
+                g, span, out_ref = finish
+                past = t + 1 - span * SKEW * (n - 1)
+
+                @pl.when((past >= chunks) & (past < all_chunks) & (lax.rem(past + chunks, chunks) == 0))
+                def _():
+                    finish_start(g, lax.div(past, chunks) - 1)
+
+                late = past - lag
+
+                @pl.when((late >= chunks) & (late < all_chunks) & (lax.rem(late + chunks, chunks) == 0))
+                def _():
+                    finish_end(g, lax.div(late, chunks) - 1, out_ref)
+
             for when, act in hooks:
 
                 @pl.when(t == when)
@@ -272,16 +303,6 @@
 
         prefetch(0, 0)
         lax.fori_loop(0, steps, step, 0)
-
-    def ends(m, span):
-        return (m + 1) * chunks - 1 + span * SKEW * (n - 1)
-
-    def finish_hooks(g, span, out_ref):
-        hooks = []
-        for m in range(micros - 1):
-            hooks.append((ends(m, span), functools.partial(finish_start, g, m)))
-            hooks.append((ends(m, span) + LAG, functools.partial(finish_end, g, m, out_ref)))
-        return hooks
 
     def send_forward(h, k):
         ag[0, h, k] = gelu_value(part[...]).astype(ag.dtype)
@@ -302,47 +323,39 @@
 
     @pl.when(seg == 0)
     def _():
-        for j in range(1, count_dp):
-            emb_copy(0, d, rem_dp(d + j)).start()
-        for m in range(micros):
-            if m == 0:
-                total[...] = emb_ref[own].astype(jnp.float32)
-            else:
-                total[...] = jnp.zeros(total.shape, total.dtype)
-            for j in range(count_dp):
-                src = rem_dp(d + j)
-                if m == 0 and j == 0:
-                    continue
-                emb_copy(m, src, src).wait_recv()
-                total[...] += inbox[micros + m, src].astype(jnp.float32)
-            xin[m, own] = total[...].astype(xin.dtype)
+        for m in range(split):
             for j in range(1, count_dp):
-                x_copy(xin.at[m, own], m, d, rem_dp(d + j), seg).start()
-        stream(0, 0, "up", "down", send_forward, finish_hooks(0, 2, acts_ref))
+                emb_copy(m, d, rem_dp(d + j)).start()
+        embed_end(0)
+        later = [((m - 1) * chunks + 1, functools.partial(embed_end, m)) for m in range(1, micros)]
+        stream(0, 0, "up", "down", send_forward, (0, 2, acts_ref), later)
         finish_start(0, last)
         finish_end(0, last, acts_ref)
-        stream(1, 1, "down", "up", send_backward, finish_hooks(1, 2, grads_ref))
+        stream(1, 1, "down", "up", send_backward, (1, 2, grads_ref))
         finish_start(1, last)
         finish_end(1, last, grads_ref)
-        for j in range(1, count_dp):
-            emb_copy(0, d, rem_dp(d + j)).wait_send()
+        for m in range(split):
+            for j in range(1, count_dp):
+                emb_copy(m, d, rem_dp(d + j)).wait_send()
 
     @pl.when(seg == 1)
     def _():
-        for j in range(count_dp):
-            emb_copy(1, d, rem_dp(d + j)).start()
+        for m in range(split):
+            for j in range(count_dp):
+                emb_copy(split + m, d, rem_dp(d + j)).start()
         for m in range(micros):
             xin[m, own] = cot_ref[m]
             for j in range(1, count_dp):
                 x_copy(cot_ref.at[m], m, d, rem_dp(d + j), seg).start()
-        stream(0, 0, "down", None, keep, [])
-        stream(1, 0, "up", "up", send_turn, finish_hooks(0, 2, grads_ref))
+        stream(0, 0, "down", None, keep)
+        stream(1, 0, "up", "up", send_turn, (0, 2, grads_ref))
         finish_start(0, last)
-        stream(1, 1, None, "down", None, [(LAG, functools.partial(finish_end, 0, last, grads_ref))] + finish_hooks(1, 1, acts_ref))
+        stream(1, 1, None, "down", None, (1, 1, acts_ref), [(lag, functools.partial(finish_end, 0, last, grads_ref))])
         finish_start(1, last)
         finish_end(1, last, acts_ref)
-        for j in range(count_dp):
-            emb_copy(1, d, rem_dp(d + j)).wait_send()
+        for m in range(split):
+            for j in range(count_dp):
+                emb_copy(split + m, d, rem_dp(d + j)).wait_send()
 
     def drain(k, carry):
         for i in range(2):
@@ -366,9 +379,9 @@
             x_copy(cot_ref.at[m], micros + m, d, rem_dp(d + j), 1 - seg).wait_send()
 
 
-def relay(emb, cotangent, w_up, w_down, count_dp, count_mp):
+def relay(emb, cotangent, w_up, w_down, split, count_dp, count_mp):
     micros, local, model = cotangent.shape
-    rows = emb.shape[0]
+    rows = emb.shape[0] // split
     hidden = w_up.shape[1]
     chunks = max(1, hidden // 2 // CHUNK)
     width = hidden // 2 // chunks
@@ -379,7 +392,7 @@
     dma = pltpu.SemaphoreType.DMA
     out = jax.ShapeDtypeStruct((micros, local, model), low)
     return pl.pallas_call(
-        functools.partial(relay_kernel, count_dp, count_mp, micros, chunks, width),
+        functools.partial(relay_kernel, count_dp, count_mp, split, chunks, width),
         out_shape=(out, out),
         in_specs=[vmem, vmem, hbm, hbm],
         out_specs=(vmem, vmem),
@@ -402,7 +415,7 @@
             dma((2 * micros, count_dp)),
             dma((2 * micros, count_dp)),
             dma((2 * micros, count_dp)),
-            dma((count_dp,)),
+            dma((split, count_dp)),
             dma((micros, count_dp)),
             dma((2, 2, 2)),
         ],
@@ -414,13 +427,18 @@
 
 def on_device(token_ids, table, w_up, w_down, cotangent):
     table_rows = table.shape[0]
+    count_dp, count_mp = lax.axis_size("dp"), lax.axis_size("mp")
+    micros, local, model = cotangent.shape
+    split = SPLIT if local % (16 * SPLIT) == 0 else 1
     ids = lax.dynamic_index_in_dim(token_ids, lax.axis_index("segment"), 0, keepdims=False)
+    ids = ids.reshape(count_dp, split, local // split).transpose(1, 0, 2).reshape(-1)
     picked = ids - lax.axis_index("dp") * table_rows
     inside = (picked >= 0) & (picked < table_rows)
     fetched = jnp.take(table, jnp.clip(picked, 0, table_rows - 1), axis=0, mode="clip")
     emb = jnp.where(inside[:, None], fetched, jnp.zeros_like(fetched))
-    acts, grads = relay(emb, cotangent, w_up[0], w_down[0], lax.axis_size("dp"), lax.axis_size("mp"))
-    return acts[None], grads[None]
+    groups = cotangent.reshape(micros * split, local // split, model)
+    acts, grads = relay(emb, groups, w_up[0], w_down[0], split, count_dp, count_mp)
+    return acts.reshape(cotangent.shape)[None], grads.reshape(cotangent.shape)[None]
 
 
 def solution(mesh):

time: 545 us -> 485 us (0.89)
  the two profiles are of different devices: /device:TPU:0 before, /device:TPU:1 now
where the time goes in v1:
time: 485 us; the launch traced here: 484 us
  Pallas kernels  466 us (96%)
  local copies, waits for them, and re-layouts  14.6 us (3%)
    pallas_call x1, Pallas kernels, relay(): pl.pallas_call(functools.partial(relay_kernel, count_dp, count_mp, split,...  466 us
    gather x1, local copies, waits for them, and re-layouts, on_device(): jnp.take(table, jnp.clip(picked, 0, table_rows - 1), axis=0, mode='clip')  10.4 us

profile of v1, /device:TPU:1, one launch (start us, length us, event | category | flops | bytes accessed | tf_op | source)
XLA Modules:
  0.0 484.1 jit_solution(9634300199409309131)
XLA Ops:
  0.6 0.7 and_reduce_fusion
  1.3 0.7 clamp_reduce_fusion
  2.0 0.1 reshape.53
  2.1 0.1 and.17
  2.2 0.1 min.16
  2.3 0.1 reshape.56
  2.4 10.4 %gather_fusion = bf16[256,2048]{1,0:T(8,128)(2,1)S(1)} fusion(bf16[8192,2048]{1,0:T(8,128)(2,1)} %param.6, s32[1024]{0:T(1024)S(1)} %pad_clamp_fusion), kind=kCustom, calls=%fused_computation | custom fusion | bytes 2098176 | tf_op jit(solution)/shard_map/jit(_take)/gather | solution.py:437
  12.9 1.1 broadcast_select_fusion.emb_ref
  14.0 466.3 %shard_map.68 = (bf16[4,32,2048]{2,1,0:T(8,128)(2,1)}, bf16[4,32,2048]{2,1,0:T(8,128)(2,1)}) custom-call(bf16[256,2048]{1,0:T(8,128)(2,1)} %broadcast_select_fusion.emb_ref, bf16[4,32,2048]{2,1,0:T(8,128)(2,1)} %bitcast.11, bf16[2048,8192]{1,0:T(8,128)(2,1)} %bitcast.9, bf16[8192,2048]{1,0:T(8,128)(2,1)} %bitcast.10), custom_call_target="tpu_custom_call" | custom-call | tf_op jit(solution)/shard_map/pallas_call | solution.py:394
  480.3 1.9 copy.13
  482.2 1.9 copy.14
  (3 shorter events, 0.0 us)
